TPU v7x, 256 devices: a whole 4x4x8 slice. The times are simulated.
256 devices in a mesh: order: 64 (over z, x, core), lat: 4 (over y).
Axes of the slice: x: 4, y: 4, z: 8, core: 2. Of those that a mesh axis runs over, the one named last changes fastest.
Arguments:
- position: float32 [128, 2, 64, 2160], P('order', None, None, 'lat'), may hold values from -6 to 6
- residual: float32 [128, 2, 64, 2160], P('order', None, None, 'lat'), as said below
- direction: float32 [128, 2, 64, 2160], P('order', None, None, 'lat'), as said below
- legendre: float32 [128, 2160, 2048], P('order', None, 'lat'), may hold values from -0.125 to 0.125
- order_of: int32 [128], replicated, may hold values from 0 to 2032, as said below
- class_idx: int32 [2048, 4320], P(('lat', 'order')), may hold values from 0 to 15
- land: int32 [2048, 4320], P(('lat', 'order')), may hold values 0 or 1
- class_weight: float32 [16, 2], replicated, may hold values from 0.2 to 5
- damping: float32 [2160], P('lat'), may hold values from 0.05 to 0.5
Outputs:
- new_position: float32 [128, 2, 64, 2160], P('order', None, None, 'lat')
- new_residual: float32 [128, 2, 64, 2160], P('order', None, None, 'lat')
- new_direction: float32 [128, 2, 64, 2160], P('order', None, None, 'lat')
Inputs may be any that keep to these rules, and one draw needn't show every extreme that they name: `order_of`: distinct multiples of 16: each of 0, 16, ..., 16 * (128 - 1) appears exactly once. `residual`: real-valued and not zero. `direction`: real-valued and not zero.
All inputs are finite; a program needn't handle non-finite values. No bound on the sum of `land` on one device may be relied on, other than what follows from the above.
Results may differ from a plain program's by a relative error of at most 0.000058.
Values sent between devices are 32-bit elements; how exact they have to be, the bound alone decides.
A program may use at most 128 MiB of HBM per device.

v0:
```python
import math
import jax
import jax.numpy as jnp
from jax import lax
from jax.sharding import PartitionSpec as P


def tables(order_of, longitudes):
    longitude = jnp.arange(longitudes, dtype=jnp.int32)
    phases = order_of[:, None] * longitude[None, :] % longitudes
    angles = phases.astype(jnp.float32) * (2.0 * math.pi / longitudes)
    return jnp.stack([jnp.cos(angles), jnp.sin(angles)])


def sample_sums(product):
    return jnp.sum(product, axis=(0, 1, 3))


def shards(
    position, residual, direction, legendre, order_of, class_idx, land, class_weight, damping
):
    highest = lax.Precision.HIGHEST
    m_local = position.shape[0]
    samples = position.shape[2]
    deg_local = position.shape[3]
    band_rows = legendre.shape[2]
    lat_index = lax.axis_index("lat")
    order_index = lax.axis_index("order")
    my_orders = lax.dynamic_slice_in_dim(order_of, order_index * m_local, m_local)
    deg_start = lat_index * deg_local
    own_degrees = deg_start + jnp.arange(deg_local, dtype=jnp.int32)
    own_valid = (own_degrees[None, :] >= my_orders[:, None]).astype(jnp.float32)[:, None, None, :]
    pos_m = position * own_valid
    res_m = residual * own_valid
    dir_m = direction * own_valid
    norm_before = lax.psum(sample_sums(res_m * res_m), ("order", "lat"))
    block_part = lax.all_gather(direction, "lat", axis=3, tiled=True)
    degree_count = block_part.shape[3]
    in_block = jnp.arange(degree_count, dtype=jnp.int32)
    in_triangle = (in_block[None, :] >= my_orders[:, None]).astype(jnp.float32)
    masked = block_part * in_triangle[:, None, None, :]
    synthesis = jnp.einsum("mskd,mdt->mtsk", masked, legendre, precision=highest)
    grid_in = lax.all_to_all(
        synthesis.reshape(m_local, band_rows, 2 * samples),
        "order",
        split_axis=1,
        concat_axis=0,
        tiled=True,
    )
    orders_all = grid_in.shape[0]
    rows_here = grid_in.shape[1]
    grid_in = grid_in.reshape(orders_all, rows_here, 2, samples)
    longitudes = class_idx.shape[1]
    harmonic = tables(order_of, longitudes)
    surface = jnp.einsum("mrsk,sml->rkl", grid_in, harmonic, precision=highest)
    class_count = class_weight.shape[0]
    onehot = (
        class_idx[:, :, None] == jnp.arange(class_count, dtype=jnp.int32)[None, None, :]
    ).astype(jnp.float32)
    by_class = jnp.dot(onehot, class_weight, precision=highest)
    weight_grid = jnp.where(land == 1, by_class[:, :, 1], by_class[:, :, 0])
    weighted = surface * weight_grid[:, None, :]
    spectra = jnp.einsum("rkl,sml->mrsk", weighted, harmonic, precision=highest) * (
        2.0 / longitudes
    )
    returned = lax.all_to_all(
        spectra.reshape(orders_all, rows_here, 2 * samples),
        "order",
        split_axis=0,
        concat_axis=1,
        tiled=True,
    )
    returned = returned.reshape(m_local, band_rows, 2, samples)
    band_part = jnp.einsum("mtsk,mdt->mskd", returned, legendre, precision=highest)
    totals = lax.psum(band_part, "lat")
    summed = lax.dynamic_slice_in_dim(totals, deg_start, deg_local, 3)
    applied = (summed + damping[None, None, None, :] * dir_m) * own_valid
    curvature_sum = lax.psum(sample_sums(dir_m * applied), ("order", "lat"))
    step_size = (norm_before / curvature_sum)[None, None, :, None]
    new_residual = res_m - step_size * applied
    norm_after = lax.psum(sample_sums(new_residual * new_residual), ("order", "lat"))
    ratio_new = (norm_after / norm_before)[None, None, :, None]
    new_position = pos_m + step_size * dir_m
    new_direction = new_residual + ratio_new * dir_m
    return (new_position, new_residual, new_direction)


def solution(mesh):
    return jax.shard_map(
        shards,
        mesh=mesh,
        in_specs=(
            P("order", None, None, "lat"),
            P("order", None, None, "lat"),
            P("order", None, None, "lat"),
            P("order", None, "lat"),
            P(),
            P(("lat", "order"), None),
            P(("lat", "order"), None),
            P(),
            P("lat"),
        ),
        out_specs=(
            P("order", None, None, "lat"),
            P("order", None, None, "lat"),
            P("order", None, None, "lat"),
        ),
        check_vma=False,
    )
```

profile of v0, /device:TPU:1, one launch (start us, length us, event | category | flops | bytes accessed | tf_op | source)
XLA Modules:
  0.0 419.9 jit_solution(14200132624685688203)
XLA Ops:
  7.2 2.3 copy.20
  9.7 0.7 fusion.11
  10.6 0.9 fusion.37
  11.4 9.9 %fusion.17 = (f32[1,128,4320]{1,2,0:T(8,128)S(1)}, f32[1,128,4320]{1,2,0:T(8,128)}) fusion(s32[128]{0:T(128)S(1)} %copy-done.10), kind=kLoop, calls=%fused_computation.23 | loop fusion | flops 4976640 | bytes 4424192 | tf_op jit(solution)/shard_map/cos | solution.py:12
  21.3 44.9 %all-gather.2.cloned.1.call-done = f32[2,2,64,2160]{2,1,0,3:T(2,128)} async-done(((f32[2,2,64,540]{2,1,0,3:T(2,128)}), f32[2,2,64,2160]{2,1,0,3:T(2,128)}) %all-gather.2.cloned.1.call-update) | async-done | bytes 2211856 | tf_op jit(solution)/shard_map/all_gather | solution.py:37
  66.2 6.6 %broadcast_multiply_fusion = f32[2,2,64,2160]{2,1,0,3:T(2,128)S(1)} fusion(f32[2,2,64,2160]{2,1,0,3:T(2,128)} %all-gather.2.cloned.1.call-done, f32[2,2160]{0,1:T(8,128)S(1)} %fusion.30), kind=kLoop, calls=%fused_computation.18 | loop fusion | flops 552960 | bytes 4440960 | tf_op jit(solution)/shard_map/mul | solution.py:41
  72.8 8.7 %fusion.4 = f32[2,2,64,512]{3,2,1,0:T(8,128)S(1)} fusion(f32[2,2160,512]{2,1,0:T(8,128)S(1)} %copy-done.1, f32[2,2,64,2160]{2,1,0,3:T(2,128)S(1)} %broadcast_multiply_fusion), kind=kOutput, calls=%fused_computation.5 | convolution fusion | flops 3397386240 | bytes 11583488 | tf_op jit(solution)/shard_map/mskd,mdt->mtsk/dot_general | solution.py:42
  81.5 1.0 copy.22
  82.5 10.8 %all-to-all-start = ((f32[2,512,128]{2,0,1:T(2,128)}), f32[2,512,128]{2,0,1:T(2,128)S(1)}, u32[]{:S(2)}, u32[]{:S(2)}) async-start(f32[2,512,128]{2,0,1:T(2,128)} %copy.22), calls=%async_computation | async-start | bytes 1048576 | tf_op jit(solution)/shard_map/all_to_all | solution.py:43
  93.6 17.4 %all-to-all-done = f32[2,512,128]{2,0,1:T(2,128)S(1)} async-done(((f32[2,512,128]{2,0,1:T(2,128)}), f32[2,512,128]{2,0,1:T(2,128)S(1)}, u32[]{:S(2)}, u32[]{:S(2)}) %all-to-all-start) | async-done | bytes 524320 | tf_op jit(solution)/shard_map/all_to_all | solution.py:43
  111.0 0.8 copy.24
  111.9 1.6 reshape.148
  113.5 31.3 %fusion.8 = f32[8,64,4320,1]{2,1,3,0:T(8,128)S(1)} fusion(f32[1,128,4320]{1,2,0:T(8,128)} %get-tuple-element.13, f32[1,128,4320]{1,2,0:T(8,128)S(1)} %get-tuple-element.12, f32[128,8,2,64]{3,2,1,0:T(2,128)S(1)} %reshape.148), kind=kOutput, calls=%fused_computation.10 | convolution fusion | flops 6795878400 | bytes 13795328 | tf_op jit(solution)/shard_map/mrsk,sml->rkl/dot_general | solution.py:55
  144.8 7.8 %fusion.24 = f32[128,8,2,64]{0,3,1,2:T(8,128)S(1)} fusion(f32[8,64,4320,1]{2,1,3,0:T(8,128)S(1)} %fusion.8, f32[8,4320]{1,0:T(8,128)S(1)} %fusion.33, f32[1,128,4320]{1,2,0:T(8,128)S(1)} %copy-done.2, f32[1,128,4320]{1,2,0:T(8,128)S(1)} %get-tuple-element.12), kind=kOutput, calls=%fused_computation.26 | convolution fusion | flops 6798221312 | bytes 13933568 | tf_op jit(solution)/shard_map/rkl,sml->mrsk/dot_general | solution.py:63
  152.7 0.2 copy.28
  153.0 23.3 %all_to_all.30 = f32[128,8,128]{2,1,0:T(8,128)S(1)} all-to-all(f32[128,8,128]{2,1,0:T(8,128)S(1)} %copy.28), channel_id=1, replica_groups=mesh['order'=64,'lat'=4] {'order'}, dimensions={0} | all-to-all | bytes 1048576 | tf_op jit(solution)/shard_map/all_to_all | solution.py:66
  176.3 0.6 reshape.150
  176.9 19.2 %fusion.2 = f32[2,2,64,2160]{3,2,1,0:T(8,128)} fusion(f32[2,2160,512]{2,1,0:T(8,128)} %param.12, f32[2,512,2,64]{3,2,1,0:T(2,128)S(1)} %reshape.150), kind=kOutput, calls=%fused_computation.3 | convolution fusion | flops 3397386240 | bytes 11583488 | tf_op jit(solution)/shard_map/mtsk,mdt->mskd/dot_general | solution.py:74
  196.3 61.3 %all-reduce.3.cloned.1.call-done = f32[2,2,64,2160]{3,2,1,0:T(8,128)} async-done(((f32[2,2,64,2160]{3,2,1,0:T(8,128)}), f32[2,2,64,2160]{3,2,1,0:T(8,128)}) %all-reduce.3.cloned.1.call-update) | async-done | bytes 2211856 | tf_op jit(solution)/shard_map/psum | solution.py:75
  257.6 1.6 multiply_reduce_fusion.1
  259.2 76.0 %all-reduce = (f32[64]{0:T(128)S(1)}, f32[64]{0:T(128)S(1)}) all-reduce(f32[64]{0:T(128)S(1)} %get-tuple-element.4, f32[64]{0:T(128)S(1)} %get-tuple-element.3), channel_id=1, replica_groups=mesh['order'=64,'lat'=4] {'order','lat'}, use_global_device_ids=true, to_apply=%region_1.0 | all-reduce | flops 128 | bytes 1024 | tf_op jit(solution)/shard_map/psum | solution.py:36
  335.1 2.5 multiply_reduce_fusion
  337.6 74.3 %psum.31 = f32[64]{0:T(128)S(1)} all-reduce(f32[64]{0:T(128)S(1)} %get-tuple-element.7), channel_id=1, replica_groups=mesh['order'=64,'lat'=4] {'order','lat'}, use_global_device_ids=true, to_apply=%region_6.7 | all-reduce | flops 64 | bytes 512 | tf_op jit(solution)/shard_map/psum | solution.py:81
  411.9 1.0 multiply_add_fusion
  (38 shorter events, 0.8 us)
Async XLA Ops:
  7.2 2.5 copy-start
  7.2 2.4 copy-start.10
  7.2 2.5 copy-start.11
  7.2 59.0 %all-gather.2.cloned.1.call-start = ((), (), s32[]{:S(2)}) async-start(), calls=%async_computation.2 | async-start | bytes 5529600 | tf_op jit(solution)/shard_map/all_gather | solution.py:37
  66.2 6.6 %copy-start.1 = (f32[2,2160,512]{2,1,0:T(8,128)S(1)}, f32[2,2160,512]{2,1,0:T(8,128)}, u32[]{:S(2)}) copy-start(f32[2,2160,512]{2,1,0:T(8,128)} %param.12) | copy-start | bytes 26542084
  72.7 20.8 %copy-start.7 = (f32[8,4320,1]{1,2,0:T(1,128)S(1)}, f32[8,4320,1]{1,2,0:T(1,128)}, u32[]{:S(2)}) copy-start(f32[8,4320,1]{1,2,0:T(1,128)} %get-tuple-element.11) | copy-start | bytes 414724
  72.8 20.8 %copy-start.8 = (s32[8,4320]{1,0:T(8,128)S(1)}, s32[8,4320]{1,0:T(8,128)}, u32[]{:S(2)}) copy-start(s32[8,4320]{1,0:T(8,128)} %param.15) | copy-start | bytes 414724
  82.5 28.5 %all-to-all-start = ((f32[2,512,128]{2,0,1:T(2,128)}), f32[2,512,128]{2,0,1:T(2,128)S(1)}, u32[]{:S(2)}, u32[]{:S(2)}) async-start(f32[2,512,128]{2,0,1:T(2,128)} %copy.22), calls=%async_computation | async-start | bytes 1048576 | tf_op jit(solution)/shard_map/all_to_all | solution.py:43
  93.3 164.3 %all-reduce.3.cloned.1.call-start = ((), (), s32[]{:S(2)}) async-start(), calls=%async_computation.3 | async-start | bytes 4456448 | tf_op jit(solution)/shard_map/psum | solution.py:75
  113.5 31.3 %copy-start.2 = (f32[1,128,4320]{1,2,0:T(8,128)S(1)}, f32[1,128,4320]{1,2,0:T(8,128)}, u32[]{:S(2)}) copy-start(f32[1,128,4320]{1,2,0:T(8,128)} %get-tuple-element.13) | copy-start | bytes 6635524
  196.2 61.4 %copy-start.3 = (f32[2,2,64,540]{3,2,1,0:T(8,128)S(1)}, f32[2,2,64,540]{3,2,1,0:T(8,128)}, u32[]{:S(2)}) copy-start(f32[2,2,64,540]{3,2,1,0:T(8,128)} %param.11) | copy-start | bytes 1658884
  196.2 61.4 %copy-start.4 = (f32[2,2,64,540]{3,2,1,0:T(8,128)S(1)}, f32[2,2,64,540]{3,2,1,0:T(8,128)}, u32[]{:S(2)}) copy-start(f32[2,2,64,540]{3,2,1,0:T(8,128)} %param.10) | copy-start | bytes 1658884
  196.2 61.4 %copy-start.9 = (f32[540]{0:T(1024)S(1)}, f32[540]{0:T(1024)}, u32[]{:S(2)}) copy-start(f32[540]{0:T(1024)} %param.17) | copy-start | bytes 6484
  196.2 138.9 %copy-start.6 = (f32[2,2,64,540]{3,2,1,0:T(8,128)S(1)}, f32[2,2,64,540]{3,2,1,0:T(8,128)}, u32[]{:S(2)}) copy-start(f32[2,2,64,540]{3,2,1,0:T(8,128)} %param.9) | copy-start | bytes 1658884
  337.6 75.3 %copy-start.5 = (f32[2,2,64,540]{3,2,1,0:T(8,128)}, f32[2,2,64,540]{3,2,1,0:T(8,128)S(1)}, u32[]{:S(2)}) copy-start(f32[2,2,64,540]{3,2,1,0:T(8,128)S(1)} %get-tuple-element.8) | copy-start | bytes 1658884
Sparse Core Ops, SparseCore 0:
  9.8 56.2 all-gather.1
  196.3 61.1 all-reduce.2
where the time goes:
time: 429 us; the launch traced here: 420 us
  blocking collectives  174 us (41%)
  waiting for transfers between devices  124 us (29%)
  matrix products  67.8 us (16%)
  other arithmetic  21.7 us (5%)
  between operations  14.5 us (3%)
  starting transfers between devices  11.1 us (3%)
  local copies, waits for them, and re-layouts  7.76 us (2%)
    psum x1, blocking collectives, shards(): norm_before = lax.psum(sample_sums(res_m * res_m), ('order', 'lat'))  76 us
    psum x1, blocking collectives, shards(): lax.psum(sample_sums(new_residual * new_residual), ('order', 'lat'))  74.3 us
    psum x1, waiting for transfers between devices, shards(): totals = lax.psum(band_part, 'lat')  61.3 us
    all_gather x1, waiting for transfers between devices, shards(): block_part = lax.all_gather(direction, 'lat', axis=3, tiled=True)  44.9 us
    dot_general x1, matrix products, shards(): surface = jnp.einsum('mrsk,sml->rkl', grid_in, harmonic, precision=highest)  31.3 us
    all_to_all x1, blocking collectives, shards(): lax.all_to_all(spectra.reshape(orders_all, rows_here, 2 * samples), 'orde...  23.3 us
    dot_general x1, matrix products, shards(): jnp.einsum('mtsk,mdt->mskd', returned, legendre, precision=highest)  19.2 us
    all_to_all x1, waiting for transfers between devices, shards(): lax.all_to_all(synthesis.reshape(m_local, band_rows, 2 * samples), 'order...  17.4 us
  transfers between devices with their start and end apart: 3, of which 3 were waited for; matrix products, arithmetic and copies ran while one was open for 3% of the time, Pallas kernels for 0%

commit v1 on v0

--- a/solution.py
+++ b/solution.py
@@ -40,12 +40,20 @@
     in_triangle = (in_block[None, :] >= my_orders[:, None]).astype(jnp.float32)
     masked = block_part * in_triangle[:, None, None, :]
     synthesis = jnp.einsum("mskd,mdt->mtsk", masked, legendre, precision=highest)
-    grid_in = lax.all_to_all(
-        synthesis.reshape(m_local, band_rows, 2 * samples),
-        "order",
-        split_axis=1,
-        concat_axis=0,
-        tiled=True,
+    grid_in = jnp.concatenate(
+        lax.all_to_all(
+            jnp.stack(
+                jnp.split(
+                    synthesis.reshape(m_local, band_rows, 2 * samples),
+                    lax.axis_size("order"),
+                    axis=1,
+                )
+            ),
+            "order",
+            0,
+            0,
+        ),
+        axis=0,
     )
     orders_all = grid_in.shape[0]
     rows_here = grid_in.shape[1]

time: 429 us -> 557 us (1.30)
  local copies, waits for them, and re-layouts: 7.76 us -> 139 us
    unnamed x25 -> x162, local copies, waits for them, and re-layouts: 2.38 us -> 129 us
    split x0 -> x4, local copies, waits for them, and re-layouts: none -> 6.47 us  [shards(): jnp.split(synthesis.reshape(m_local, band_rows, 2 * samples), lax.axis_si...]
  transfers between devices with their start and end apart: 3 -> 3, of which waited for: 3 -> 3; matrix products, arithmetic and copies ran while one was open for 3% -> 2% of each run, Pallas kernels for 0% -> 0%
where the time goes in v1:
time: 557 us; the launch traced here: 552 us
  blocking collectives  174 us (31%)
  local copies, waits for them, and re-layouts  139 us (25%)
  waiting for transfers between devices  122 us (22%)
  matrix products  67.6 us (12%)
  other arithmetic  22.8 us (4%)
  between operations  14.8 us (3%)
  starting transfers between devices  11.6 us (2%)
    unnamed x162, local copies, waits for them, and re-layouts  129 us
    psum x1, blocking collectives, shards(): norm_before = lax.psum(sample_sums(res_m * res_m), ('order', 'lat'))  76 us
    psum x1, blocking collectives, shards(): lax.psum(sample_sums(new_residual * new_residual), ('order', 'lat'))  74.3 us
    psum x1, waiting for transfers between devices, shards(): totals = lax.psum(band_part, 'lat')  61.3 us
    all_gather x1, waiting for transfers between devices, shards(): block_part = lax.all_gather(direction, 'lat', axis=3, tiled=True)  44.9 us
    dot_general x1, matrix products, shards(): surface = jnp.einsum('mrsk,sml->rkl', grid_in, harmonic, precision=highest)  31 us
    all_to_all x1, blocking collectives, shards(): lax.all_to_all(spectra.reshape(orders_all, rows_here, 2 * samples), 'orde...  23.4 us
    dot_general x1, matrix products, shards(): jnp.einsum('mtsk,mdt->mskd', returned, legendre, precision=highest)  19.3 us
  transfers between devices with their start and end apart: 3, of which 3 were waited for; matrix products, arithmetic and copies ran while one was open for 2% of the time, Pallas kernels for 0%

profile of v1, /device:TPU:1, one launch (start us, length us, event | category | flops | bytes accessed | tf_op | source)
XLA Modules:
  0.0 552.0 jit_solution(15473635999809441217)
XLA Ops:
  7.2 2.3 copy.90
  11.4 9.8 %fusion.17 = (f32[1,128,4320]{1,2,0:T(8,128)S(1)}, f32[1,128,4320]{1,2,0:T(8,128)}) fusion(s32[128]{0:T(128)S(1)} %copy-done.15), kind=kLoop, calls=%fused_computation.23 | loop fusion | flops 4976640 | bytes 4424192 | tf_op jit(solution)/shard_map/cos | solution.py:12
  21.3 44.9 %all-gather.2.cloned.1.call-done = f32[2,2,64,2160]{2,1,0,3:T(2,128)} async-done(((f32[2,2,64,540]{2,1,0,3:T(2,128)}), f32[2,2,64,2160]{2,1,0,3:T(2,128)}) %all-gather.2.cloned.1.call-update) | async-done | bytes 2211856 | tf_op jit(solution)/shard_map/all_gather | solution.py:37
  66.2 6.8 %broadcast_multiply_fusion = f32[2,2,64,2160]{2,1,0,3:T(2,128)S(1)} fusion(f32[2,2,64,2160]{2,1,0,3:T(2,128)} %all-gather.2.cloned.1.call-done, f32[2,2160]{0,1:T(8,128)S(1)} %fusion.30), kind=kLoop, calls=%fused_computation.18 | loop fusion | flops 552960 | bytes 4440960 | tf_op jit(solution)/shard_map/mul | solution.py:41
  73.0 8.7 %fusion.4 = f32[2,2,64,512]{3,2,1,0:T(8,128)S(1)} fusion(f32[2,2160,512]{2,1,0:T(8,128)S(1)} %copy-done.1, f32[2,2,64,2160]{2,1,0,3:T(2,128)S(1)} %broadcast_multiply_fusion), kind=kOutput, calls=%fused_computation.5 | convolution fusion | flops 3397386240 | bytes 11583488 | tf_op jit(solution)/shard_map/mskd,mdt->mtsk/dot_general | solution.py:42
  82.0 2.0 fusion.39
  84.0 2.1 fusion.38
  86.1 2.1 fusion.37
  103.8 1.6 copy.180
  122.6 1.6 copy.192
  124.2 1.6 copy.193
  127.4 1.6 copy.195
  129.0 1.6 copy.196
  215.1 11.0 %all-to-all-start = ((f32[64,2,8,128]{3,2,1,0:T(8,128)}), f32[64,2,8,128]{3,2,1,0:T(8,128)}, u32[]{:S(2)}, u32[]{:S(2)}) async-start(f32[64,2,8,128]{3,2,1,0:T(8,128)} %constant_dynamic-update-slice_fusion), calls=%async_computation | async-start | bytes 1048576 | tf_op jit(solution)/shard_map/all_to_all | solution.py:44
  227.6 16.1 %all-to-all-done = f32[64,2,8,128]{3,2,1,0:T(8,128)} async-done(((f32[64,2,8,128]{3,2,1,0:T(8,128)}), f32[64,2,8,128]{3,2,1,0:T(8,128)}, u32[]{:S(2)}, u32[]{:S(2)}) %all-to-all-start) | async-done | bytes 524320 | tf_op jit(solution)/shard_map/all_to_all | solution.py:44
  243.8 1.6 reshape_reshape.3
  245.4 31.0 %fusion.8 = f32[8,64,4320,1]{2,1,3,0:T(8,128)S(1)} fusion(f32[1,128,4320]{1,2,0:T(8,128)} %get-tuple-element.77, f32[1,128,4320]{1,2,0:T(8,128)S(1)} %get-tuple-element.76, f32[128,8,2,64]{3,2,1,0:T(2,128)S(1)} %reshape_reshape.3), kind=kOutput, calls=%fused_computation.10 | convolution fusion | flops 6795878400 | bytes 13795328 | tf_op jit(solution)/shard_map/mrsk,sml->rkl/dot_general | solution.py:63
  276.5 7.8 %fusion.24 = f32[128,8,2,64]{0,3,1,2:T(8,128)S(1)} fusion(f32[8,64,4320,1]{2,1,3,0:T(8,128)S(1)} %fusion.8, f32[8,4320]{1,0:T(8,128)S(1)} %fusion.33, f32[1,128,4320]{1,2,0:T(8,128)S(1)} %copy-done.2, f32[1,128,4320]{1,2,0:T(8,128)S(1)} %get-tuple-element.76), kind=kOutput, calls=%fused_computation.26 | convolution fusion | flops 6798221312 | bytes 13933568 | tf_op jit(solution)/shard_map/rkl,sml->mrsk/dot_general | solution.py:71
  284.6 23.4 %all_to_all.20 = f32[128,8,128]{2,1,0:T(8,128)S(1)} all-to-all(f32[128,8,128]{2,1,0:T(8,128)S(1)} %copy.159), channel_id=1, replica_groups=mesh['order'=64,'lat'=4] {'order'}, dimensions={0} | all-to-all | bytes 1048576 | tf_op jit(solution)/shard_map/all_to_all | solution.py:74
  308.7 19.3 %fusion.2 = f32[2,2,64,2160]{3,2,1,0:T(8,128)} fusion(f32[2,2160,512]{2,1,0:T(8,128)} %param.12, f32[2,512,2,64]{3,2,1,0:T(2,128)S(1)} %reshape.145), kind=kOutput, calls=%fused_computation.3 | convolution fusion | flops 3397386240 | bytes 11583488 | tf_op jit(solution)/shard_map/mtsk,mdt->mskd/dot_general | solution.py:82
  328.1 61.3 %all-reduce.3.cloned.1.call-done = f32[2,2,64,2160]{3,2,1,0:T(8,128)} async-done(((f32[2,2,64,2160]{3,2,1,0:T(8,128)}), f32[2,2,64,2160]{3,2,1,0:T(8,128)}) %all-reduce.3.cloned.1.call-update) | async-done | bytes 2211856 | tf_op jit(solution)/shard_map/psum | solution.py:83
  391.0 76.0 %all-reduce = (f32[64]{0:T(128)S(1)}, f32[64]{0:T(128)S(1)}) all-reduce(f32[64]{0:T(128)S(1)} %get-tuple-element.4, f32[64]{0:T(128)S(1)} %get-tuple-element.3), channel_id=1, replica_groups=mesh['order'=64,'lat'=4] {'order','lat'}, use_global_device_ids=true, to_apply=%region_1.0 | all-reduce | flops 128 | bytes 1024 | tf_op jit(solution)/shard_map/psum | solution.py:36
  466.9 2.5 multiply_reduce_fusion
  469.4 74.3 %psum.31 = f32[64]{0:T(128)S(1)} all-reduce(f32[64]{0:T(128)S(1)} %get-tuple-element.7), channel_id=1, replica_groups=mesh['order'=64,'lat'=4] {'order','lat'}, use_global_device_ids=true, to_apply=%region_6.7 | all-reduce | flops 64 | bytes 512 | tf_op jit(solution)/shard_map/psum | solution.py:89
  (177 shorter events, 126.1 us)
Async XLA Ops:
  7.2 2.5 copy-start
  7.2 2.4 copy-start.15
  7.2 2.5 copy-start.16
  7.2 59.0 %all-gather.2.cloned.1.call-start = ((), (), s32[]{:S(2)}) async-start(), calls=%async_computation.2 | async-start | bytes 5529600 | tf_op jit(solution)/shard_map/all_gather | solution.py:37
  66.2 6.8 %copy-start.1 = (f32[2,2160,512]{2,1,0:T(8,128)S(1)}, f32[2,2160,512]{2,1,0:T(8,128)}, u32[]{:S(2)}) copy-start(f32[2,2160,512]{2,1,0:T(8,128)} %param.12) | copy-start | bytes 26542084
  103.8 41.5 %copy-start.13 = (f32[2,8,128]{1,2,0:T(8,128)S(1)}, f32[2,8,128]{1,2,0:T(8,128)}, u32[]{:S(2)}) copy-start(f32[2,8,128]{1,2,0:T(8,128)} %get-tuple-element.27) | copy-start | bytes 24580
  122.6 33.4 %copy-start.12 = (f32[2,8,128]{1,2,0:T(8,128)S(1)}, f32[2,8,128]{1,2,0:T(8,128)}, u32[]{:S(2)}) copy-start(f32[2,8,128]{1,2,0:T(8,128)} %get-tuple-element.15) | copy-start | bytes 24580
  124.2 31.9 %copy-start.11 = (f32[2,8,128]{1,2,0:T(8,128)S(1)}, f32[2,8,128]{1,2,0:T(8,128)}, u32[]{:S(2)}) copy-start(f32[2,8,128]{1,2,0:T(8,128)} %get-tuple-element.14) | copy-start | bytes 24580
  125.8 30.4 %copy-start.10 = (f32[2,8,128]{1,2,0:T(8,128)S(1)}, f32[2,8,128]{1,2,0:T(8,128)}, u32[]{:S(2)}) copy-start(f32[2,8,128]{1,2,0:T(8,128)} %get-tuple-element.13) | copy-start | bytes 24580
  127.4 28.8 %copy-start.9 = (f32[2,8,128]{1,2,0:T(8,128)S(1)}, f32[2,8,128]{1,2,0:T(8,128)}, u32[]{:S(2)}) copy-start(f32[2,8,128]{1,2,0:T(8,128)} %get-tuple-element.12) | copy-start | bytes 24580
  129.0 27.3 %copy-start.8 = (f32[2,8,128]{1,2,0:T(8,128)S(1)}, f32[2,8,128]{1,2,0:T(8,128)}, u32[]{:S(2)}) copy-start(f32[2,8,128]{1,2,0:T(8,128)} %get-tuple-element.11) | copy-start | bytes 24580
  145.3 81.4 %copy-start.7 = (f32[8,4320,1]{1,2,0:T(1,128)S(1)}, f32[8,4320,1]{1,2,0:T(1,128)}, u32[]{:S(2)}) copy-start(f32[8,4320,1]{1,2,0:T(1,128)} %get-tuple-element.75) | copy-start | bytes 414724
  215.1 28.6 %all-to-all-start = ((f32[64,2,8,128]{3,2,1,0:T(8,128)}), f32[64,2,8,128]{3,2,1,0:T(8,128)}, u32[]{:S(2)}, u32[]{:S(2)}) async-start(f32[64,2,8,128]{3,2,1,0:T(8,128)} %constant_dynamic-update-slice_fusion), calls=%async_computation | async-start | bytes 1048576 | tf_op jit(solution)/shard_map/all_to_all | solution.py:44
  226.2 163.2 %all-reduce.3.cloned.1.call-start = ((), (), s32[]{:S(2)}) async-start(), calls=%async_computation.3 | async-start | bytes 4456448 | tf_op jit(solution)/shard_map/psum | solution.py:83
  245.4 31.1 %copy-start.2 = (f32[1,128,4320]{1,2,0:T(8,128)S(1)}, f32[1,128,4320]{1,2,0:T(8,128)}, u32[]{:S(2)}) copy-start(f32[1,128,4320]{1,2,0:T(8,128)} %get-tuple-element.77) | copy-start | bytes 6635524
  328.0 61.4 %copy-start.3 = (f32[2,2,64,540]{3,2,1,0:T(8,128)S(1)}, f32[2,2,64,540]{3,2,1,0:T(8,128)}, u32[]{:S(2)}) copy-start(f32[2,2,64,540]{3,2,1,0:T(8,128)} %param.11) | copy-start | bytes 1658884
  328.0 61.4 %copy-start.4 = (f32[2,2,64,540]{3,2,1,0:T(8,128)S(1)}, f32[2,2,64,540]{3,2,1,0:T(8,128)}, u32[]{:S(2)}) copy-start(f32[2,2,64,540]{3,2,1,0:T(8,128)} %param.10) | copy-start | bytes 1658884
  328.0 61.4 %copy-start.14 = (f32[540]{0:T(1024)S(1)}, f32[540]{0:T(1024)}, u32[]{:S(2)}) copy-start(f32[540]{0:T(1024)} %param.17) | copy-start | bytes 6484
  328.0 138.9 %copy-start.6 = (f32[2,2,64,540]{3,2,1,0:T(8,128)S(1)}, f32[2,2,64,540]{3,2,1,0:T(8,128)}, u32[]{:S(2)}) copy-start(f32[2,2,64,540]{3,2,1,0:T(8,128)} %param.9) | copy-start | bytes 1658884
  469.4 75.3 %copy-start.5 = (f32[2,2,64,540]{3,2,1,0:T(8,128)}, f32[2,2,64,540]{3,2,1,0:T(8,128)S(1)}, u32[]{:S(2)}) copy-start(f32[2,2,64,540]{3,2,1,0:T(8,128)S(1)} %get-tuple-element.8) | copy-start | bytes 1658884
Sparse Core Ops, SparseCore 0:
  9.8 56.2 all-gather.1
  328.1 61.1 all-reduce.2
